TPU v7x, 32 devices: a whole 2x2x4 slice. The times are simulated.
32 devices in a mesh: wall: 4 (over y, core), surf: 8 (over z, x).
Axes of the slice: x: 2, y: 2, z: 4, core: 2. Of those that a mesh axis runs over, the one named last changes fastest.
Arguments:
- vector: bfloat16 [32, 16, 320, 256], P('surf', 'wall'), may hold values from -40 to 40
- lengths: int32 [32], P('surf'), may hold values from 1 to 16, as said below
- north_of: int32 [8, 4], P('surf'), may hold values from 0 to 3, each once within a row
- diagonal: bfloat16 [32, 16, 320, 320], P('surf', 'wall'), may hold values from -1 to 8
- lifting: bfloat16 [32, 16, 6, 80, 320], P('surf', 'wall'), may hold values from -0.625 to 0.625
- inverse_rows: bfloat16 [32, 16, 80, 320], P('surf', 'wall'), may hold values from -0.25 to 0.25
Outputs:
- next_basis: bfloat16 [32, 16, 320, 256], P('surf', 'wall')
- coefs: float32 [2, 256], replicated
Inputs may be any that keep to these rules, and one draw needn't show every extreme that they name: `lengths`: in every patch of 4 lines one line has 16 elements and another has 1.
All inputs are finite; a program needn't handle non-finite values.
Results may differ from a plain program's by a relative error of at most 0.00135.
Values may be sent and summed in bfloat16 or wider, within the bound.
A program may use at most 64 MiB of HBM per device.

v0:
```python
import jax
import jax.numpy as jnp
from jax import lax
from jax.sharding import PartitionSpec as P

VARS = 5
NODE1D = 4
FACE = 80
FULL_ACCURACY = lax.Precision.HIGHEST


def with_halo(cells, sides, width, closed):
    for axis, dim in sides:
        count = lax.axis_size(axis)
        ends = count if closed else count - 1
        head = lax.slice_in_dim(cells, 0, width, axis=dim)
        tail = lax.slice_in_dim(cells, cells.shape[dim] - width, cells.shape[dim], axis=dim)
        cells = jnp.concatenate(
            [
                lax.ppermute(tail, axis, [(i, (i + 1) % count) for i in range(ends)]),
                cells,
                lax.ppermute(head, axis, [((i + 1) % count, i) for i in range(ends)]),
            ],
            axis=dim,
        )
    return cells


def from_behind(shard, axis, by):
    devices = lax.axis_size(axis)
    pairs = [(i, i + by) for i in range(devices) if 0 <= i + by < devices]
    return lax.ppermute(shard, axis, pairs)


def face_traces(values):
    leading = values.shape[:-2]
    column_entries = values.shape[-1]
    nodal_cube = values.reshape(leading + (VARS, NODE1D, NODE1D, NODE1D, column_entries))
    last_node = NODE1D - 1

    def flatten(piece):
        return piece.reshape(leading + (FACE, column_entries))

    bottom_face = flatten(nodal_cube[..., 0, :])
    top_face = flatten(nodal_cube[..., last_node, :])
    west_face = flatten(nodal_cube[..., 0, :, :, :])
    east_face = flatten(nodal_cube[..., last_node, :, :, :])
    south_face = flatten(nodal_cube[..., 0, :, :])
    north_face = flatten(nodal_cube[..., last_node, :, :])
    return (bottom_face, top_face, west_face, east_face, south_face, north_face)


def exact_times(form, left, right):
    return jnp.einsum(
        form, left.astype(jnp.float32), right.astype(jnp.float32), precision=FULL_ACCURACY
    )


def apply_map(matrices, states):
    return exact_times("lfg,lgr->lfr", matrices, states)


def per_device(vector, lengths, north_of, diagonal, lifting, inverse_rows):
    lines_here, segment, block_size, column_entries = vector.shape
    face_size = inverse_rows.shape[2]
    positions = lax.axis_index("wall") * segment + jnp.arange(segment, dtype=jnp.int32)
    alive_mask = positions[None, :] < lengths[:, None]
    living = alive_mask.astype(jnp.float32)
    masked = vector * alive_mask.astype(jnp.bfloat16)[:, :, None, None]
    bottom_face, top_face, west_face, east_face, south_face, north_face = face_traces(masked)
    wall_edges = jnp.stack([bottom_face[:, 0], top_face[:, -1]], axis=1)
    wall_padded = with_halo(wall_edges, (("wall", 1),), 1, False)
    from_below = jnp.concatenate([wall_padded[:, 0:1], top_face[:, :-1]], axis=1)
    from_above = jnp.concatenate([bottom_face[:, 1:], wall_padded[:, 3:4]], axis=1)
    patch_edges = jnp.stack([west_face[0], east_face[-1]], axis=0)
    patch_padded = with_halo(patch_edges, (("surf", 0),), 1, True)
    from_west = jnp.concatenate([patch_padded[0:1], east_face[:-1]], axis=0)
    from_east = jnp.concatenate([west_face[1:], patch_padded[3:4]], axis=0)
    selector = (north_of[0][:, None] == jnp.arange(lines_here, dtype=jnp.int32)[None, :]).astype(
        jnp.bfloat16
    )
    from_north = jnp.einsum(
        "ij,jsfr->isfr", selector, south_face, preferred_element_type=jnp.float32
    ).astype(jnp.bfloat16)
    from_south = jnp.einsum(
        "ij,isfr->jsfr", selector, north_face, preferred_element_type=jnp.float32
    ).astype(jnp.bfloat16)
    neighbours = jnp.stack(
        [from_below, from_above, from_west, from_east, from_south, from_north], axis=2
    )
    matrix_product = jnp.einsum(
        "lsbc,lscr->lsbr", diagonal, masked, preferred_element_type=jnp.float32
    )
    matrix_product = matrix_product + jnp.einsum(
        "lsgfb,lsgfr->lsbr", lifting, neighbours, preferred_element_type=jnp.float32
    )
    matrix_product = matrix_product * living[:, :, None, None]
    lower_lift = lifting[:, :, 0]
    identity_map = jnp.broadcast_to(
        jnp.eye(face_size, dtype=jnp.float32), (lines_here, face_size, face_size)
    )
    carried = jnp.zeros((lines_here, face_size, column_entries), jnp.float32)
    prefix = identity_map
    free_part = []
    prefixes = []
    for position in range(segment):
        alive_now = living[:, position][:, None, None]
        eliminated = alive_now * (
            matrix_product[:, position]
            - exact_times("lfb,lfr->lbr", lower_lift[:, position], carried)
        )
        free_part.append(eliminated)
        prefixes.append(prefix)
        carried = exact_times("lfb,lbr->lfr", inverse_rows[:, position], eliminated)
        step_map = -alive_now * exact_times(
            "lfb,lgb->lfg", inverse_rows[:, position], lower_lift[:, position]
        )
        prefix = exact_times("lfg,lgh->lfh", step_map, prefix)
    whole_map = prefix
    offset = carried
    wall_count = lax.axis_size("wall")

    def advance(turn_index, received):
        outgoing = apply_map(whole_map, received) + offset
        return from_behind(outgoing, "wall", 1)

    incoming = lax.fori_loop(0, wall_count - 1, advance, jnp.zeros_like(offset))
    finished = []
    for position in range(segment):
        alive_now = living[:, position][:, None, None]
        arriving = apply_map(prefixes[position], incoming)
        correction = exact_times("lfb,lfr->lbr", lower_lift[:, position], arriving)
        finished.append(free_part[position] - alive_now * correction)
    eliminated = jnp.stack(finished, axis=1)
    masked_wide = masked.astype(jnp.float32)
    entries = lines_here * segment * block_size * lax.axis_size("surf") * lax.axis_size("wall")
    coupling_total, self_sum = lax.psum(
        (
            jnp.sum(masked_wide * eliminated, axis=(0, 1, 2)),
            jnp.sum(masked_wide * masked_wide, axis=(0, 1, 2)),
        ),
        ("wall", "surf"),
    )
    projection = coupling_total / self_sum
    remainder = eliminated - projection * masked_wide
    squares = lax.psum(jnp.sum(remainder * remainder, axis=(0, 1, 2)), ("wall", "surf"))
    spread = jnp.sqrt(squares / entries + 1e-06)
    next_basis = (remainder / spread).astype(jnp.bfloat16)
    return (next_basis, jnp.stack([projection, spread]))


def solution(mesh):
    in_specs = (
        P("surf", "wall", None, None),
        P("surf"),
        P("surf", None),
        P("surf", "wall", None, None),
        P("surf", "wall", None, None, None),
        P("surf", "wall", None, None),
    )
    out_specs = (P("surf", "wall", None, None), P())
    return jax.shard_map(
        per_device, mesh=mesh, in_specs=in_specs, out_specs=out_specs, check_vma=False
    )
```

profile of v0, /device:TPU:0, one launch (start us, length us, event | category | flops | bytes accessed | tf_op | source)
XLA Modules:
  0.0 194.8 jit_solution(14934975038232348811)
XLA Ops:
  0.6 0.7 compare_convert_fusion.1
  1.4 3.5 %copy_multiply_fusion = bf16[4,4,320,256]{3,2,0,1:T(8,128)(2,1)} fusion(bf16[4,4,320,256]{3,2,1,0:T(8,128)(2,1)} %param.8, bf16[4,4]{0,1:T(4,128)(2,1)S(1)} %get-tuple-element.58), kind=kLoop, calls=%fused_computation.17 | loop fusion | flops 1310720 | bytes 5242912 | tf_op jit(solution)/shard_map/mul | solution.py:69
  4.8 3.5 %reshape.104 = bf16[4,4,5,4,4,4,256]{6,5,4,3,2,0,1:T(4,128)(2,1)S(1)} reshape(bf16[4,4,320,256]{3,2,0,1:T(8,128)(2,1)} %copy_multiply_fusion) | data formatting | bytes 5242880 | tf_op jit(solution)/shard_map/reshape | solution.py:38
  8.4 3.0 %fusion.77 = (bf16[4,4,5,4,4,1,256]{6,5,4,3,2,0,1:T(2,128)(2,1)S(1)}, bf16[4,4,5,4,4,1,256]{6,5,4,3,2,0,1:T(2,128)(2,1)S(1)}) fusion(bf16[4,4,5,4,4,4,256]{6,5,4,3,2,0,1:T(4,128)(2,1)S(1)} %reshape.104), kind=kLoop, calls=%fused_computation.121 | loop fusion | bytes 2621440 | tf_op jit(solution)/shard_map/slice | solution.py:44
  11.4 1.0 copy.27
  12.4 0.7 slice.155
  13.1 3.1 %collective-permute-start.1 = (bf16[4,1,80,256]{3,0,2,1:T(4,128)(2,1)}, bf16[4,1,80,256]{3,0,2,1:T(4,128)(2,1)}, u32[]{:S(2)}, u32[]{:S(2)}) collective-permute-start(bf16[4,1,80,256]{3,0,2,1:T(4,128)(2,1)} %slice.155), channel_id=1, source_target_pairs={{0,8},{8,16},{16,24},{1,9},{9,17},{17,25},{2,10},{10,18},{18,26},{... | collective-permute-start | bytes 491528 | tf_op jit(solution)/shard_map/ppermute | solution.py:20
  16.1 1.0 copy.28
  17.1 0.7 slice.159
  17.9 1.3 collective-permute-start.2
  19.4 1.0 copy.30
  20.4 2.3 %collective-permute-start.3 = (bf16[1,4,80,256]{3,0,2,1:T(2,128)(2,1)}, bf16[1,4,80,256]{3,0,2,1:T(2,128)(2,1)}, u32[]{:S(2)}, u32[]{:S(2)}) collective-permute-start(bf16[1,4,80,256]{3,0,2,1:T(2,128)(2,1)} %copy.30), channel_id=1, source_target_pairs={{0,1},{1,2},{2,3},{3,4},{4,5},{5,6},{6,7},{7,0},{8,9},{9,10},{10,1... | collective-permute-start | bytes 491528 | tf_op jit(solution)/shard_map/ppermute | solution.py:20
  22.8 1.0 copy.34
  23.8 3.0 %collective-permute-start.4 = (bf16[1,4,80,256]{3,0,2,1:T(2,128)(2,1)}, bf16[1,4,80,256]{3,0,2,1:T(2,128)(2,1)}, u32[]{:S(2)}, u32[]{:S(2)}) collective-permute-start(bf16[1,4,80,256]{3,0,2,1:T(2,128)(2,1)} %copy.34), channel_id=1, source_target_pairs={{1,0},{2,1},{3,2},{4,3},{5,4},{6,5},{7,6},{0,7},{9,8},{10,9},{11,1... | collective-permute-start | bytes 491528 | tf_op jit(solution)/shard_map/ppermute | solution.py:22
  26.8 1.4 fusion.75
  28.2 1.4 fusion.74
  29.6 1.3 copy_bitcast_fusion
  33.1 0.9 slice.156
  34.1 1.0 slice.158
  35.1 1.2 copy.31
  36.3 1.4 copy.32
  37.7 1.2 copy.35
  38.9 1.2 copy.37
  40.1 1.3 fusion.35
  41.5 1.5 fusion.36
  43.0 1.7 fusion.37
  44.8 1.7 fusion.38
  46.5 0.8 fusion.32
  47.4 0.7 fusion.34
  48.1 4.8 %fusion.5 = f32[4,4,256,320,1]{2,3,4,1,0:T(8,128)S(1)} fusion(bf16[4,4,6,80,320]{4,3,2,1,0:T(8,128)(2,1)} %param.12, bf16[4,4,6,80,256]{4,0,3,1,2:T(4,128)(2,1)S(1)} %fusion.34), kind=kOutput, calls=%fused_computation.13 | convolution fusion | flops 1258291200 | bytes 14090240 | tf_op jit(solution)/shard_map/lsgfb,lsgfr->lsbr/dot_general | solution.py:94
  52.9 3.7 %fusion.4 = f32[4,4,320,256]{3,2,1,0:T(8,128)S(1)} fusion(f32[4,4,256,320,1]{2,3,4,1,0:T(8,128)S(1)} %fusion.5, f32[4,4]{1,0:T(4,128)S(1)} %copy.39, bf16[4,4,320,320]{3,2,1,0:T(8,128)(2,1)} %param.11, bf16[4,4,320,256]{3,2,0,1:T(8,128)(2,1)S(1)} %copy-done.1), kind=kOutput, calls=%fused_computation.10 | convolution fusion | flops 841482240 | bytes 16384064 | tf_op jit(solution)/shard_map/lsbc,lscr->lsbr/dot_general | solution.py:91
  57.2 0.6 copy-done.20
  57.8 0.8 fusion.41
  58.7 1.8 fusion.28
  60.5 0.7 fusion.44
  61.2 0.8 fusion.26
  62.0 0.7 fusion.47
  63.1 0.8 fusion.24
  63.9 1.0 copy-done.6
  64.9 0.7 convolution_bitcast_fusion.4
  65.7 25.3 %while.10 = (s32[]{:T(128)}, f32[4,80,256]{2,1,0:T(8,128)S(1)}, f32[4,80,80]{2,1,0:T(8,128)S(1)}, f32[4,80,256]{2,1,0:T(8,128)S(1)}, s32[]{:T(128)}) while((s32[]{:T(128)}, f32[4,80,256]{2,1,0:T(8,128)S(1)}, f32[4,80,80]{2,1,0:T(8,128)S(1)}, f32[4,80,256]{2,1,0:T(8,128)S(1)}, s32[]{:T(128)}) %tuple.36), condition=%wide.region_1.0_spmd, body=%wide.region_0.0_spmd.sunk | while | flops 78725120 | bytes 2396261 | solution.py:127
  65.7 1.1 convolution_add_fusion.2
  66.8 3.4 %collective-permute-start = (f32[4,80,256]{2,1,0:T(8,128)}, f32[4,80,256]{2,1,0:T(8,128)S(1)}, u32[]{:S(2)}, u32[]{:S(2)}) collective-permute-start(f32[4,80,256]{2,1,0:T(8,128)} %convolution_add_fusion.2), channel_id=1, source_target_pairs={{0,8},{8,16},{16,24},{1,9},{9,17},{17,25},{2,10},{10,18},{18,26},{... | collective-permute-start | bytes 983048 | tf_op jit(solution)/shard_map/while/body/eval_jaxpr/ppermute | solution.py:32
  70.3 1.4 collective-permute-done
  71.7 1.1 convolution_add_fusion.2
  72.8 7.0 %collective-permute-start = (f32[4,80,256]{2,1,0:T(8,128)}, f32[4,80,256]{2,1,0:T(8,128)S(1)}, u32[]{:S(2)}, u32[]{:S(2)}) collective-permute-start(f32[4,80,256]{2,1,0:T(8,128)} %convolution_add_fusion.2), channel_id=1, source_target_pairs={{0,8},{8,16},{16,24},{1,9},{9,17},{17,25},{2,10},{10,18},{18,26},{... | collective-permute-start | bytes 983048 | tf_op jit(solution)/shard_map/while/body/eval_jaxpr/ppermute | solution.py:32
  79.8 1.4 collective-permute-done
  81.2 1.1 convolution_add_fusion.2
  82.4 7.2 %collective-permute-start = (f32[4,80,256]{2,1,0:T(8,128)}, f32[4,80,256]{2,1,0:T(8,128)S(1)}, u32[]{:S(2)}, u32[]{:S(2)}) collective-permute-start(f32[4,80,256]{2,1,0:T(8,128)} %convolution_add_fusion.2), channel_id=1, source_target_pairs={{0,8},{8,16},{16,24},{1,9},{9,17},{17,25},{2,10},{10,18},{18,26},{... | collective-permute-start | bytes 983048 | tf_op jit(solution)/shard_map/while/body/eval_jaxpr/ppermute | solution.py:32
  89.6 1.4 collective-permute-done
  91.4 1.3 fusion.81
  92.7 1.3 fusion.82
  94.1 1.3 fusion.83
  95.4 0.8 fusion.16
  96.2 0.8 fusion.18
  97.0 0.8 fusion.20
  98.2 0.8 fusion.22
  99.6 1.6 fusion.1
  101.2 43.8 %all-reduce = (f32[256]{0:T(256)S(1)}, f32[256]{0:T(256)S(1)}) all-reduce(f32[256]{0:T(256)S(1)} %get-tuple-element.30, f32[256]{0:T(256)S(1)} %get-tuple-element.29), channel_id=1, replica_groups=mesh['wall'=4,'surf'=8] {'wall','surf'}, use_global_device_ids=true, to_apply=%region_3.0 | all-reduce | flops 512 | bytes 4096 | tf_op jit(solution)/shard_map/psum | solution.py:137
  145.0 3.1 %multiply_reduce_fusion = f32[256]{0:T(256)S(1)} fusion(f32[256]{0:T(256)S(1)} %div.17, f32[4,1,320,256]{3,2,0,1:T(8,128)} %copy-done.5, f32[4,1,320,256]{3,2,0,1:T(8,128)} %copy-done.4, f32[4,1,320,256]{3,2,0,1:T(8,128)} %copy-done.3, f32[4,1,320,256]{3,2,0,1:T(8,128)} %copy-done.2, bf16[4,4]{0,1:T(4,128)(2,1)S(1)} %get-tuple-element.58, ...), kind=kLoop, calls=%fused_computation.12 | loop fusion | flops 11796224 | bytes 7866400 | tf_op jit(solution)/shard_map/reduce_sum | solution.py:146
  148.1 41.3 %psum.23 = f32[256]{0:T(256)S(1)} all-reduce(f32[256]{0:T(256)S(1)} %multiply_reduce_fusion), channel_id=1, replica_groups=mesh['wall'=4,'surf'=8] {'wall','surf'}, use_global_device_ids=true, to_apply=%region_7.0 | all-reduce | flops 256 | bytes 2048 | tf_op jit(solution)/shard_map/psum | solution.py:146
  189.5 3.0 %divide_convert_fusion = bf16[4,4,320,256]{3,2,0,1:T(8,128)(2,1)S(1)} fusion(f32[256]{0:T(256)S(1)} %add_sqrt_fusion, f32[256]{0:T(256)S(1)} %div.17, f32[4,1,320,256]{3,2,0,1:T(8,128)} %copy-done.5, f32[4,1,320,256]{3,2,0,1:T(8,128)} %copy-done.4, f32[4,1,320,256]{3,2,0,1:T(8,128)} %copy-done.3, f32[4,1,320,256]{3,2,0,1:T(8,128)} %copy-done.2, ...), kind=kLoop, calls=%fused_computation.11 | loop fusion | flops 11796480 | bytes 10487840 | tf_op jit(solution)/shard_map/convert_element_type | solution.py:148
  192.5 1.7 copy.45
  194.2 0.6 pad_maximum_fusion.1
  (71 shorter events, 4.9 us)
Async XLA Ops:
  13.1 27.0 %collective-permute-start.1 = (bf16[4,1,80,256]{3,0,2,1:T(4,128)(2,1)}, bf16[4,1,80,256]{3,0,2,1:T(4,128)(2,1)}, u32[]{:S(2)}, u32[]{:S(2)}) collective-permute-start(bf16[4,1,80,256]{3,0,2,1:T(4,128)(2,1)} %slice.155), channel_id=1, source_target_pairs={{0,8},{8,16},{16,24},{1,9},{9,17},{17,25},{2,10},{10,18},{18,26},{... | collective-permute-start | bytes 491528 | tf_op jit(solution)/shard_map/ppermute | solution.py:20
  17.9 23.6 %collective-permute-start.2 = (bf16[4,1,80,256]{3,0,2,1:T(4,128)(2,1)}, bf16[4,1,80,256]{3,0,2,1:T(4,128)(2,1)}, u32[]{:S(2)}, u32[]{:S(2)}) collective-permute-start(bf16[4,1,80,256]{3,0,2,1:T(4,128)(2,1)} %slice.159), channel_id=1, source_target_pairs={{8,0},{16,8},{24,16},{9,1},{17,9},{25,17},{10,2},{18,10},{26,18},{... | collective-permute-start | bytes 491528 | tf_op jit(solution)/shard_map/ppermute | solution.py:22
  20.4 22.7 %collective-permute-start.3 = (bf16[1,4,80,256]{3,0,2,1:T(2,128)(2,1)}, bf16[1,4,80,256]{3,0,2,1:T(2,128)(2,1)}, u32[]{:S(2)}, u32[]{:S(2)}) collective-permute-start(bf16[1,4,80,256]{3,0,2,1:T(2,128)(2,1)} %copy.30), channel_id=1, source_target_pairs={{0,1},{1,2},{2,3},{3,4},{4,5},{5,6},{6,7},{7,0},{8,9},{9,10},{10,1... | collective-permute-start | bytes 491528 | tf_op jit(solution)/shard_map/ppermute | solution.py:20
  23.8 21.0 %collective-permute-start.4 = (bf16[1,4,80,256]{3,0,2,1:T(2,128)(2,1)}, bf16[1,4,80,256]{3,0,2,1:T(2,128)(2,1)}, u32[]{:S(2)}, u32[]{:S(2)}) collective-permute-start(bf16[1,4,80,256]{3,0,2,1:T(2,128)(2,1)} %copy.34), channel_id=1, source_target_pairs={{1,0},{2,1},{3,2},{4,3},{5,4},{6,5},{7,6},{0,7},{9,8},{10,9},{11,1... | collective-permute-start | bytes 491528 | tf_op jit(solution)/shard_map/ppermute | solution.py:22
  28.2 2.8 %copy-start.19 = (bf16[4,4,80,320]{3,2,1,0:T(8,128)(2,1)S(1)}, bf16[4,4,80,320]{3,2,1,0:T(8,128)(2,1)}, u32[]{:S(2)}) copy-start(bf16[4,4,80,320]{3,2,1,0:T(8,128)(2,1)} %param.13) | copy-start | bytes 2457604
  30.9 25.7 %copy-start.10 = (bf16[4,4,80,320]{3,2,0,1:T(8,128)(2,1)}, bf16[4,4,80,320]{3,2,0,1:T(8,128)(2,1)S(1)}, u32[]{:S(2)}) copy-start(bf16[4,4,80,320]{3,2,0,1:T(8,128)(2,1)S(1)} %copy_bitcast_fusion) | copy-start | bytes 2457604
  31.4 3.7 %copy-start.15 = (bf16[3,4,5,1,4,4,256]{6,5,4,3,2,0,1:T(4,128)(2,1)S(1)}, bf16[3,4,5,1,4,4,256]{6,5,4,3,2,0,1:T(4,128)(2,1)}, u32[]{:S(2)}) copy-start(bf16[3,4,5,1,4,4,256]{6,5,4,3,2,0,1:T(4,128)(2,1)} %get-tuple-element.44) | copy-start | bytes 1474564
  32.2 4.2 %copy-start.16 = (f32[4,80,80]{2,1,0:T(8,128)}, f32[4,80,80]{2,1,0:T(8,128)S(1)}, u32[]{:S(2)}) copy-start(f32[4,80,80]{2,1,0:T(8,128)S(1)} %fusion.61) | copy-start | bytes 307204
  32.5 5.2 %copy-start.17 = (f32[4,80,80]{2,1,0:T(8,128)}, f32[4,80,80]{2,1,0:T(8,128)S(1)}, u32[]{:S(2)}) copy-start(f32[4,80,80]{2,1,0:T(8,128)S(1)} %fusion.78) | copy-start | bytes 307204
  32.5 5.2 %copy-start.13 = (bf16[4,4,5,4,1,4,256]{6,5,4,3,2,0,1:T(4,128)(2,1)S(1)}, bf16[4,4,5,4,1,4,256]{6,5,4,3,2,0,1:T(4,128)(2,1)}, u32[]{:S(2)}) copy-start(bf16[4,4,5,4,1,4,256]{6,5,4,3,2,0,1:T(4,128)(2,1)} %get-tuple-element.42) | copy-start | bytes 1966084
  32.8 6.1 %copy-start.18 = (f32[4,80,80]{2,1,0:T(8,128)}, f32[4,80,80]{2,1,0:T(8,128)S(1)}, u32[]{:S(2)}) copy-start(f32[4,80,80]{2,1,0:T(8,128)S(1)} %fusion.79) | copy-start | bytes 307204
  38.9 4.1 %copy-start.14 = (bf16[3,4,5,1,4,4,256]{6,0,5,4,2,1,3:T(4,128)(2,1)S(1)}, bf16[3,4,5,1,4,4,256]{6,0,5,4,2,1,3:T(4,128)(2,1)}, u32[]{:S(2)}) copy-start(bf16[3,4,5,1,4,4,256]{6,0,5,4,2,1,3:T(4,128)(2,1)} %copy.31) | copy-start | bytes 1474564
  41.5 5.0 %copy-start.21 = (bf16[4,4,5,4,1,4,256]{6,0,5,3,2,1,4:T(4,128)(2,1)S(1)}, bf16[4,4,5,4,1,4,256]{6,0,5,3,2,1,4:T(4,128)(2,1)}, u32[]{:S(2)}) copy-start(bf16[4,4,5,4,1,4,256]{6,0,5,3,2,1,4:T(4,128)(2,1)} %copy.35) | copy-start | bytes 1966084
  41.5 5.0 %copy-start.23 = (s32[1,4]{1,0:T(1,128)S(1)}, s32[1,4]{1,0:T(1,128)}, u32[]{:S(2)}) copy-start(s32[1,4]{1,0:T(1,128)} %param.10) | copy-start | bytes 52
  43.0 4.4 %copy-start.22 = (bf16[4,4,5,4,1,4,256]{6,0,5,3,2,1,4:T(4,128)(2,1)S(1)}, bf16[4,4,5,4,1,4,256]{6,0,5,3,2,1,4:T(4,128)(2,1)}, u32[]{:S(2)}) copy-start(bf16[4,4,5,4,1,4,256]{6,0,5,3,2,1,4:T(4,128)(2,1)} %copy.37) | copy-start | bytes 1966084
  48.1 4.8 %copy-start.1 = (bf16[4,4,320,256]{3,2,0,1:T(8,128)(2,1)S(1)}, bf16[4,4,320,256]{3,2,0,1:T(8,128)(2,1)}, u32[]{:S(2)}) copy-start(bf16[4,4,320,256]{3,2,0,1:T(8,128)(2,1)} %copy_multiply_fusion) | copy-start | bytes 7864324
  56.6 1.2 copy-start.20
  58.7 2.5 %copy-start.11 = (bf16[4,4,80,320]{3,2,0,1:T(8,128)(2,1)S(1)}, bf16[4,4,80,320]{3,2,0,1:T(8,128)(2,1)}, u32[]{:S(2)}) copy-start(bf16[4,4,80,320]{3,2,0,1:T(8,128)(2,1)} %copy-done.10) | copy-start | bytes 2457604
  62.0 1.1 copy-start.8
  63.9 1.1 copy-start.6
  66.8 4.8 %collective-permute-start = (f32[4,80,256]{2,1,0:T(8,128)}, f32[4,80,256]{2,1,0:T(8,128)S(1)}, u32[]{:S(2)}, u32[]{:S(2)}) collective-permute-start(f32[4,80,256]{2,1,0:T(8,128)} %convolution_add_fusion.2), channel_id=1, source_target_pairs={{0,8},{8,16},{16,24},{1,9},{9,17},{17,25},{2,10},{10,18},{18,26},{... | collective-permute-start | bytes 983048 | tf_op jit(solution)/shard_map/while/body/eval_jaxpr/ppermute | solution.py:32
  72.8 8.4 %collective-permute-start = (f32[4,80,256]{2,1,0:T(8,128)}, f32[4,80,256]{2,1,0:T(8,128)S(1)}, u32[]{:S(2)}, u32[]{:S(2)}) collective-permute-start(f32[4,80,256]{2,1,0:T(8,128)} %convolution_add_fusion.2), channel_id=1, source_target_pairs={{0,8},{8,16},{16,24},{1,9},{9,17},{17,25},{2,10},{10,18},{18,26},{... | collective-permute-start | bytes 983048 | tf_op jit(solution)/shard_map/while/body/eval_jaxpr/ppermute | solution.py:32
  82.4 8.6 %collective-permute-start = (f32[4,80,256]{2,1,0:T(8,128)}, f32[4,80,256]{2,1,0:T(8,128)S(1)}, u32[]{:S(2)}, u32[]{:S(2)}) collective-permute-start(f32[4,80,256]{2,1,0:T(8,128)} %convolution_add_fusion.2), channel_id=1, source_target_pairs={{0,8},{8,16},{16,24},{1,9},{9,17},{17,25},{2,10},{10,18},{18,26},{... | collective-permute-start | bytes 983048 | tf_op jit(solution)/shard_map/while/body/eval_jaxpr/ppermute | solution.py:32
  91.0 4.4 %copy-start.12 = (bf16[4,4,80,320]{3,2,0,1:T(8,128)(2,1)S(1)}, bf16[4,4,80,320]{3,2,0,1:T(8,128)(2,1)}, u32[]{:S(2)}) copy-start(bf16[4,4,80,320]{3,2,0,1:T(8,128)(2,1)} %copy-done.10) | copy-start | bytes 2457604
  95.4 1.6 copy-start.9
  96.2 2.8 %copy-start.2 = (f32[4,1,320,256]{3,2,0,1:T(8,128)}, f32[4,1,320,256]{3,2,0,1:T(8,128)S(1)}, u32[]{:S(2)}) copy-start(f32[4,1,320,256]{3,2,0,1:T(8,128)S(1)} %fusion.16) | copy-start | bytes 3932164
  96.2 2.0 %copy-start.7 = (f32[4,320,256]{2,1,0:T(8,128)S(1)}, f32[4,320,256]{2,1,0:T(8,128)}, u32[]{:S(2)}) copy-start(f32[4,320,256]{2,1,0:T(8,128)} %copy-done.6) | copy-start | bytes 3932164
  97.0 2.0 %copy-start.3 = (f32[4,1,320,256]{3,2,0,1:T(8,128)}, f32[4,1,320,256]{3,2,0,1:T(8,128)S(1)}, u32[]{:S(2)}) copy-start(f32[4,1,320,256]{3,2,0,1:T(8,128)S(1)} %fusion.18) | copy-start | bytes 3932164
  97.0 2.6 %copy-start = (bf16[4,4,320,256]{3,2,1,0:T(8,128)(2,1)S(1)}, bf16[4,4,320,256]{3,2,1,0:T(8,128)(2,1)}, u32[]{:S(2)}) copy-start(bf16[4,4,320,256]{3,2,1,0:T(8,128)(2,1)} %param.8) | copy-start | bytes 7864324
  98.2 2.9 %copy-start.4 = (f32[4,1,320,256]{3,2,0,1:T(8,128)}, f32[4,1,320,256]{3,2,0,1:T(8,128)S(1)}, u32[]{:S(2)}) copy-start(f32[4,1,320,256]{3,2,0,1:T(8,128)S(1)} %fusion.20) | copy-start | bytes 3932164
  99.6 1.6 copy-start.5
where the time goes:
time: 196 us; the launch traced here: 195 us
  blocking collectives  85.1 us (43%)
  matrix products  29.9 us (15%)
  local copies, waits for them, and re-layouts  28.1 us (14%)
  starting transfers between devices  27.2 us (14%)
  other arithmetic  18.8 us (10%)
  waiting for transfers between devices  4.28 us (2%)
    psum x1, blocking collectives, per_device(): lax.psum((jnp.sum(masked_wide * eliminated, axis=(0, 1, 2)), jnp.sum(mask...  43.8 us
    psum x1, blocking collectives, per_device(): lax.psum(jnp.sum(remainder * remainder, axis=(0, 1, 2)), ('wall', 'surf'))  41.3 us
    dot_general x27, matrix products, exact_times(): jnp.einsum(form, left.astype(jnp.float32), right.astype(jnp.float32), pre...  19.8 us
    ppermute x3, starting transfers between devices, from_behind(): return lax.ppermute(shard, axis, pairs)  17.6 us
    unnamed x4, other arithmetic  6.28 us
    ppermute x2, starting transfers between devices, with_halo(): lax.ppermute(tail, axis, [(i, (i + 1) % count) for i in range(ends)])  5.37 us
    unnamed x51, local copies, waits for them, and re-layouts  4.98 us
    dot_general x1, matrix products, per_device(): jnp.einsum('lsgfb,lsgfr->lsbr', lifting, neighbours, preferred_element_ty...  4.77 us
  transfers between devices with their start and end apart: 7, of which 3 were waited for; matrix products, arithmetic and copies ran while one was open for 11% of the time, Pallas kernels for 0%

commit v1 on v0

--- a/solution.py
+++ b/solution.py
@@ -135,11 +135,14 @@
     masked_wide = masked.astype(jnp.float32)
     entries = lines_here * segment * block_size * lax.axis_size("surf") * lax.axis_size("wall")
     coupling_total, self_sum = lax.psum(
-        (
-            jnp.sum(masked_wide * eliminated, axis=(0, 1, 2)),
-            jnp.sum(masked_wide * masked_wide, axis=(0, 1, 2)),
+        lax.psum(
+            (
+                jnp.sum(masked_wide * eliminated, axis=(0, 1, 2)),
+                jnp.sum(masked_wide * masked_wide, axis=(0, 1, 2)),
+            ),
+            "surf",
         ),
-        ("wall", "surf"),
+        "wall",
     )
     projection = coupling_total / self_sum
     remainder = eliminated - projection * masked_wide

time: 196 us -> 179 us (0.913)
  blocking collectives: 85.1 us -> 67.2 us
    psum x1, blocking collectives: 43.8 us -> 19 us  [per_device(): lax.psum((jnp.sum(masked_wide * eliminated, axis=(0, 1, 2)), jnp.sum(mask...]
    psum x0 -> x1, blocking collectives: none -> 11 us  [per_device(): lax.psum(lax.psum((jnp.sum(masked_wide * eliminated, axis=(0, 1, 2)), jnp...]
    psum x1, blocking collectives: 41.3 us -> 37.2 us  [per_device(): lax.psum(jnp.sum(remainder * remainder, axis=(0, 1, 2)), ('wall', 'surf'))]
  transfers between devices with their start and end apart: 7 -> 7, of which waited for: 3 -> 3; matrix products, arithmetic and copies ran while one was open for 11% -> 12% of each run, Pallas kernels for 0% -> 0%
where the time goes in v1:
time: 179 us; the launch traced here: 177 us
  blocking collectives  67.2 us (38%)
  matrix products  29.9 us (17%)
  local copies, waits for them, and re-layouts  28.1 us (16%)
  starting transfers between devices  27.2 us (15%)
  other arithmetic  18.8 us (11%)
  waiting for transfers between devices  4.28 us (2%)
    psum x1, blocking collectives, per_device(): lax.psum(jnp.sum(remainder * remainder, axis=(0, 1, 2)), ('wall', 'surf'))  37.2 us
    dot_general x27, matrix products, exact_times(): jnp.einsum(form, left.astype(jnp.float32), right.astype(jnp.float32), pre...  19.9 us
    psum x1, blocking collectives, per_device(): lax.psum((jnp.sum(masked_wide * eliminated, axis=(0, 1, 2)), jnp.sum(mask...  19 us
    ppermute x3, starting transfers between devices, from_behind(): return lax.ppermute(shard, axis, pairs)  17.5 us
    psum x1, blocking collectives, per_device(): lax.psum(lax.psum((jnp.sum(masked_wide * eliminated, axis=(0, 1, 2)), jnp...  11 us
    unnamed x4, other arithmetic  6.28 us
    ppermute x2, starting transfers between devices, with_halo(): lax.ppermute(tail, axis, [(i, (i + 1) % count) for i in range(ends)])  5.38 us
    unnamed x51, local copies, waits for them, and re-layouts  4.98 us
  transfers between devices with their start and end apart: 7, of which 3 were waited for; matrix products, arithmetic and copies ran while one was open for 12% of the time, Pallas kernels for 0%

profile of v1, /device:TPU:0, one launch (start us, length us, event | category | flops | bytes accessed | tf_op | source)
XLA Modules:
  0.0 176.9 jit_solution(1757926929309873719)
XLA Ops:
  0.6 0.7 compare_convert_fusion.1
  1.4 3.5 %copy_multiply_fusion = bf16[4,4,320,256]{3,2,0,1:T(8,128)(2,1)} fusion(bf16[4,4,320,256]{3,2,1,0:T(8,128)(2,1)} %param.8, bf16[4,4]{0,1:T(4,128)(2,1)S(1)} %get-tuple-element.60), kind=kLoop, calls=%fused_computation.17 | loop fusion | flops 1310720 | bytes 5242912 | tf_op jit(solution)/shard_map/mul | solution.py:69
  4.8 3.5 %reshape.104 = bf16[4,4,5,4,4,4,256]{6,5,4,3,2,0,1:T(4,128)(2,1)S(1)} reshape(bf16[4,4,320,256]{3,2,0,1:T(8,128)(2,1)} %copy_multiply_fusion) | data formatting | bytes 5242880 | tf_op jit(solution)/shard_map/reshape | solution.py:38
  8.4 3.0 %fusion.77 = (bf16[4,4,5,4,4,1,256]{6,5,4,3,2,0,1:T(2,128)(2,1)S(1)}, bf16[4,4,5,4,4,1,256]{6,5,4,3,2,0,1:T(2,128)(2,1)S(1)}) fusion(bf16[4,4,5,4,4,4,256]{6,5,4,3,2,0,1:T(4,128)(2,1)S(1)} %reshape.104), kind=kLoop, calls=%fused_computation.121 | loop fusion | bytes 2621440 | tf_op jit(solution)/shard_map/slice | solution.py:44
  11.4 1.0 copy.27
  12.4 0.7 slice.155
  13.1 3.1 %collective-permute-start.1 = (bf16[4,1,80,256]{3,0,2,1:T(4,128)(2,1)}, bf16[4,1,80,256]{3,0,2,1:T(4,128)(2,1)}, u32[]{:S(2)}, u32[]{:S(2)}) collective-permute-start(bf16[4,1,80,256]{3,0,2,1:T(4,128)(2,1)} %slice.155), channel_id=1, source_target_pairs={{0,8},{8,16},{16,24},{1,9},{9,17},{17,25},{2,10},{10,18},{18,26},{... | collective-permute-start | bytes 491528 | tf_op jit(solution)/shard_map/ppermute | solution.py:20
  16.2 1.0 copy.28
  17.2 0.7 slice.159
  17.9 1.3 collective-permute-start.2
  19.4 1.0 copy.30
  20.4 2.3 %collective-permute-start.3 = (bf16[1,4,80,256]{3,0,2,1:T(2,128)(2,1)}, bf16[1,4,80,256]{3,0,2,1:T(2,128)(2,1)}, u32[]{:S(2)}, u32[]{:S(2)}) collective-permute-start(bf16[1,4,80,256]{3,0,2,1:T(2,128)(2,1)} %copy.30), channel_id=1, source_target_pairs={{0,1},{1,2},{2,3},{3,4},{4,5},{5,6},{6,7},{7,0},{8,9},{9,10},{10,1... | collective-permute-start | bytes 491528 | tf_op jit(solution)/shard_map/ppermute | solution.py:20
  22.8 1.0 copy.34
  23.8 3.0 %collective-permute-start.4 = (bf16[1,4,80,256]{3,0,2,1:T(2,128)(2,1)}, bf16[1,4,80,256]{3,0,2,1:T(2,128)(2,1)}, u32[]{:S(2)}, u32[]{:S(2)}) collective-permute-start(bf16[1,4,80,256]{3,0,2,1:T(2,128)(2,1)} %copy.34), channel_id=1, source_target_pairs={{1,0},{2,1},{3,2},{4,3},{5,4},{6,5},{7,6},{0,7},{9,8},{10,9},{11,1... | collective-permute-start | bytes 491528 | tf_op jit(solution)/shard_map/ppermute | solution.py:22
  26.8 1.4 fusion.75
  28.2 1.4 fusion.74
  29.6 1.3 copy_bitcast_fusion
  33.2 1.0 slice.156
  34.1 1.0 slice.158
  35.2 1.2 copy.31
  36.4 1.4 copy.32
  37.8 1.2 copy.35
  39.0 1.2 copy.37
  40.2 1.3 fusion.35
  41.5 1.5 fusion.36
  43.1 1.7 fusion.37
  44.8 1.7 fusion.38
  46.5 0.8 fusion.32
  47.4 0.7 fusion.34
  48.1 4.8 %fusion.5 = f32[4,4,256,320,1]{2,3,4,1,0:T(8,128)S(1)} fusion(bf16[4,4,6,80,320]{4,3,2,1,0:T(8,128)(2,1)} %param.12, bf16[4,4,6,80,256]{4,0,3,1,2:T(4,128)(2,1)S(1)} %fusion.34), kind=kOutput, calls=%fused_computation.13 | convolution fusion | flops 1258291200 | bytes 14090240 | tf_op jit(solution)/shard_map/lsgfb,lsgfr->lsbr/dot_general | solution.py:94
  52.9 3.7 %fusion.4 = f32[4,4,320,256]{3,2,1,0:T(8,128)S(1)} fusion(f32[4,4,256,320,1]{2,3,4,1,0:T(8,128)S(1)} %fusion.5, f32[4,4]{1,0:T(4,128)S(1)} %copy.39, bf16[4,4,320,320]{3,2,1,0:T(8,128)(2,1)} %param.11, bf16[4,4,320,256]{3,2,0,1:T(8,128)(2,1)S(1)} %copy-done.1), kind=kOutput, calls=%fused_computation.10 | convolution fusion | flops 841482240 | bytes 16384064 | tf_op jit(solution)/shard_map/lsbc,lscr->lsbr/dot_general | solution.py:91
  57.2 0.6 copy-done.20
  57.9 0.8 fusion.41
  58.7 1.8 %fusion.28 = f32[4,320,256]{2,1,0:T(8,128)S(1)} fusion(f32[4,256,80]{1,2,0:T(8,128)S(1)} %fusion.41, f32[4,4,320,256]{3,2,1,0:T(8,128)S(1)} %fusion.4, f32[4]{0:T(128)S(1)} %get-tuple-element.56, bf16[4,4,80,320]{3,2,0,1:T(8,128)(2,1)} %copy-done.10), kind=kOutput, calls=%fused_computation.42 | convolution fusion | flops 315228160 | bytes 3194896 | tf_op jit(solution)/shard_map/lfb,lfr->lbr/dot_general | solution.py:54
  60.5 0.7 fusion.44
  61.3 0.8 fusion.26
  62.1 0.7 fusion.47
  63.1 0.8 fusion.24
  63.9 1.0 copy-done.6
  65.0 0.7 convolution_bitcast_fusion.4
  65.7 25.3 %while.10 = (s32[]{:T(128)}, f32[4,80,256]{2,1,0:T(8,128)S(1)}, f32[4,80,80]{2,1,0:T(8,128)S(1)}, f32[4,80,256]{2,1,0:T(8,128)S(1)}, s32[]{:T(128)}) while((s32[]{:T(128)}, f32[4,80,256]{2,1,0:T(8,128)S(1)}, f32[4,80,80]{2,1,0:T(8,128)S(1)}, f32[4,80,256]{2,1,0:T(8,128)S(1)}, s32[]{:T(128)}) %tuple.36), condition=%wide.region_1.0_spmd, body=%wide.region_0.0_spmd.sunk | while | flops 78725120 | bytes 2396261 | solution.py:127
  65.7 1.1 convolution_add_fusion.2
  66.9 3.4 %collective-permute-start = (f32[4,80,256]{2,1,0:T(8,128)}, f32[4,80,256]{2,1,0:T(8,128)S(1)}, u32[]{:S(2)}, u32[]{:S(2)}) collective-permute-start(f32[4,80,256]{2,1,0:T(8,128)} %convolution_add_fusion.2), channel_id=1, source_target_pairs={{0,8},{8,16},{16,24},{1,9},{9,17},{17,25},{2,10},{10,18},{18,26},{... | collective-permute-start | bytes 983048 | tf_op jit(solution)/shard_map/while/body/eval_jaxpr/ppermute | solution.py:32
  70.3 1.4 collective-permute-done
  71.7 1.1 convolution_add_fusion.2
  72.9 7.0 %collective-permute-start = (f32[4,80,256]{2,1,0:T(8,128)}, f32[4,80,256]{2,1,0:T(8,128)S(1)}, u32[]{:S(2)}, u32[]{:S(2)}) collective-permute-start(f32[4,80,256]{2,1,0:T(8,128)} %convolution_add_fusion.2), channel_id=1, source_target_pairs={{0,8},{8,16},{16,24},{1,9},{9,17},{17,25},{2,10},{10,18},{18,26},{... | collective-permute-start | bytes 983048 | tf_op jit(solution)/shard_map/while/body/eval_jaxpr/ppermute | solution.py:32
  79.9 1.4 collective-permute-done
  81.3 1.1 convolution_add_fusion.2
  82.4 7.2 %collective-permute-start = (f32[4,80,256]{2,1,0:T(8,128)}, f32[4,80,256]{2,1,0:T(8,128)S(1)}, u32[]{:S(2)}, u32[]{:S(2)}) collective-permute-start(f32[4,80,256]{2,1,0:T(8,128)} %convolution_add_fusion.2), channel_id=1, source_target_pairs={{0,8},{8,16},{16,24},{1,9},{9,17},{17,25},{2,10},{10,18},{18,26},{... | collective-permute-start | bytes 983048 | tf_op jit(solution)/shard_map/while/body/eval_jaxpr/ppermute | solution.py:32
  89.6 1.4 collective-permute-done
  91.4 1.3 fusion.81
  92.8 1.3 fusion.82
  94.1 1.3 fusion.83
  95.5 0.8 fusion.16
  96.3 0.8 fusion.18
  97.1 0.8 fusion.20
  98.3 0.8 fusion.22
  99.7 1.6 fusion.1
  101.2 19.0 %all-reduce = (f32[256]{0:T(256)S(1)}, f32[256]{0:T(256)S(1)}) all-reduce(f32[256]{0:T(256)S(1)} %get-tuple-element.30, f32[256]{0:T(256)S(1)} %get-tuple-element.29), channel_id=1, replica_groups=mesh['wall'=4,'surf'=8] {'surf'}, use_global_device_ids=true, to_apply=%region_3.0 | all-reduce | flops 512 | bytes 4096 | tf_op jit(solution)/shard_map/psum | solution.py:138
  120.2 11.0 %all-reduce.1 = (f32[256]{0:T(256)S(1)}, f32[256]{0:T(256)S(1)}) all-reduce(f32[256]{0:T(256)S(1)} %get-tuple-element.39, f32[256]{0:T(256)S(1)} %get-tuple-element.40), channel_id=1, replica_groups=mesh['wall'=4,'surf'=8] {'wall'}, use_global_device_ids=true, to_apply=%region_4.0 | all-reduce | flops 512 | bytes 4096 | tf_op jit(solution)/shard_map/psum | solution.py:137
  131.2 3.1 %multiply_reduce_fusion = f32[256]{0:T(256)S(1)} fusion(f32[256]{0:T(256)S(1)} %div.17, f32[4,1,320,256]{3,2,0,1:T(8,128)} %copy-done.5, f32[4,1,320,256]{3,2,0,1:T(8,128)} %copy-done.4, f32[4,1,320,256]{3,2,0,1:T(8,128)} %copy-done.3, f32[4,1,320,256]{3,2,0,1:T(8,128)} %copy-done.2, bf16[4,4]{0,1:T(4,128)(2,1)S(1)} %get-tuple-element.60, ...), kind=kLoop, calls=%fused_computation.12 | loop fusion | flops 11796224 | bytes 7866400 | tf_op jit(solution)/shard_map/reduce_sum | solution.py:149
  134.4 37.2 %psum.39 = f32[256]{0:T(256)S(1)} all-reduce(f32[256]{0:T(256)S(1)} %multiply_reduce_fusion), channel_id=1, replica_groups=mesh['wall'=4,'surf'=8] {'wall','surf'}, use_global_device_ids=true, to_apply=%region_9.0 | all-reduce | flops 256 | bytes 2048 | tf_op jit(solution)/shard_map/psum | solution.py:149
  171.6 3.0 %divide_convert_fusion = bf16[4,4,320,256]{3,2,0,1:T(8,128)(2,1)S(1)} fusion(f32[256]{0:T(256)S(1)} %add_sqrt_fusion, f32[256]{0:T(256)S(1)} %div.17, f32[4,1,320,256]{3,2,0,1:T(8,128)} %copy-done.5, f32[4,1,320,256]{3,2,0,1:T(8,128)} %copy-done.4, f32[4,1,320,256]{3,2,0,1:T(8,128)} %copy-done.3, f32[4,1,320,256]{3,2,0,1:T(8,128)} %copy-done.2, ...), kind=kLoop, calls=%fused_computation.11 | loop fusion | flops 11796480 | bytes 10487840 | tf_op jit(solution)/shard_map/convert_element_type | solution.py:151
  174.6 1.7 copy.45
  (72 shorter events, 5.5 us)
Async XLA Ops:
  13.1 27.1 %collective-permute-start.1 = (bf16[4,1,80,256]{3,0,2,1:T(4,128)(2,1)}, bf16[4,1,80,256]{3,0,2,1:T(4,128)(2,1)}, u32[]{:S(2)}, u32[]{:S(2)}) collective-permute-start(bf16[4,1,80,256]{3,0,2,1:T(4,128)(2,1)} %slice.155), channel_id=1, source_target_pairs={{0,8},{8,16},{16,24},{1,9},{9,17},{17,25},{2,10},{10,18},{18,26},{... | collective-permute-start | bytes 491528 | tf_op jit(solution)/shard_map/ppermute | solution.py:20
  17.9 23.7 %collective-permute-start.2 = (bf16[4,1,80,256]{3,0,2,1:T(4,128)(2,1)}, bf16[4,1,80,256]{3,0,2,1:T(4,128)(2,1)}, u32[]{:S(2)}, u32[]{:S(2)}) collective-permute-start(bf16[4,1,80,256]{3,0,2,1:T(4,128)(2,1)} %slice.159), channel_id=1, source_target_pairs={{8,0},{16,8},{24,16},{9,1},{17,9},{25,17},{10,2},{18,10},{26,18},{... | collective-permute-start | bytes 491528 | tf_op jit(solution)/shard_map/ppermute | solution.py:22
  20.4 22.7 %collective-permute-start.3 = (bf16[1,4,80,256]{3,0,2,1:T(2,128)(2,1)}, bf16[1,4,80,256]{3,0,2,1:T(2,128)(2,1)}, u32[]{:S(2)}, u32[]{:S(2)}) collective-permute-start(bf16[1,4,80,256]{3,0,2,1:T(2,128)(2,1)} %copy.30), channel_id=1, source_target_pairs={{0,1},{1,2},{2,3},{3,4},{4,5},{5,6},{6,7},{7,0},{8,9},{9,10},{10,1... | collective-permute-start | bytes 491528 | tf_op jit(solution)/shard_map/ppermute | solution.py:20
  23.8 21.1 %collective-permute-start.4 = (bf16[1,4,80,256]{3,0,2,1:T(2,128)(2,1)}, bf16[1,4,80,256]{3,0,2,1:T(2,128)(2,1)}, u32[]{:S(2)}, u32[]{:S(2)}) collective-permute-start(bf16[1,4,80,256]{3,0,2,1:T(2,128)(2,1)} %copy.34), channel_id=1, source_target_pairs={{1,0},{2,1},{3,2},{4,3},{5,4},{6,5},{7,6},{0,7},{9,8},{10,9},{11,1... | collective-permute-start | bytes 491528 | tf_op jit(solution)/shard_map/ppermute | solution.py:22
  28.2 2.8 %copy-start.19 = (bf16[4,4,80,320]{3,2,1,0:T(8,128)(2,1)S(1)}, bf16[4,4,80,320]{3,2,1,0:T(8,128)(2,1)}, u32[]{:S(2)}) copy-start(bf16[4,4,80,320]{3,2,1,0:T(8,128)(2,1)} %param.13) | copy-start | bytes 2457604
  30.9 25.7 %copy-start.10 = (bf16[4,4,80,320]{3,2,0,1:T(8,128)(2,1)}, bf16[4,4,80,320]{3,2,0,1:T(8,128)(2,1)S(1)}, u32[]{:S(2)}) copy-start(bf16[4,4,80,320]{3,2,0,1:T(8,128)(2,1)S(1)} %copy_bitcast_fusion) | copy-start | bytes 2457604
  31.4 3.7 %copy-start.15 = (bf16[3,4,5,1,4,4,256]{6,5,4,3,2,0,1:T(4,128)(2,1)S(1)}, bf16[3,4,5,1,4,4,256]{6,5,4,3,2,0,1:T(4,128)(2,1)}, u32[]{:S(2)}) copy-start(bf16[3,4,5,1,4,4,256]{6,5,4,3,2,0,1:T(4,128)(2,1)} %get-tuple-element.46) | copy-start | bytes 1474564
  32.2 4.1 %copy-start.16 = (f32[4,80,80]{2,1,0:T(8,128)}, f32[4,80,80]{2,1,0:T(8,128)S(1)}, u32[]{:S(2)}) copy-start(f32[4,80,80]{2,1,0:T(8,128)S(1)} %fusion.61) | copy-start | bytes 307204
  32.5 5.2 %copy-start.17 = (f32[4,80,80]{2,1,0:T(8,128)}, f32[4,80,80]{2,1,0:T(8,128)S(1)}, u32[]{:S(2)}) copy-start(f32[4,80,80]{2,1,0:T(8,128)S(1)} %fusion.78) | copy-start | bytes 307204
  32.5 5.2 %copy-start.13 = (bf16[4,4,5,4,1,4,256]{6,5,4,3,2,0,1:T(4,128)(2,1)S(1)}, bf16[4,4,5,4,1,4,256]{6,5,4,3,2,0,1:T(4,128)(2,1)}, u32[]{:S(2)}) copy-start(bf16[4,4,5,4,1,4,256]{6,5,4,3,2,0,1:T(4,128)(2,1)} %get-tuple-element.44) | copy-start | bytes 1966084
  32.8 6.1 %copy-start.18 = (f32[4,80,80]{2,1,0:T(8,128)}, f32[4,80,80]{2,1,0:T(8,128)S(1)}, u32[]{:S(2)}) copy-start(f32[4,80,80]{2,1,0:T(8,128)S(1)} %fusion.79) | copy-start | bytes 307204
  39.0 4.1 %copy-start.14 = (bf16[3,4,5,1,4,4,256]{6,0,5,4,2,1,3:T(4,128)(2,1)S(1)}, bf16[3,4,5,1,4,4,256]{6,0,5,4,2,1,3:T(4,128)(2,1)}, u32[]{:S(2)}) copy-start(bf16[3,4,5,1,4,4,256]{6,0,5,4,2,1,3:T(4,128)(2,1)} %copy.31) | copy-start | bytes 1474564
  41.5 5.0 %copy-start.21 = (bf16[4,4,5,4,1,4,256]{6,0,5,3,2,1,4:T(4,128)(2,1)S(1)}, bf16[4,4,5,4,1,4,256]{6,0,5,3,2,1,4:T(4,128)(2,1)}, u32[]{:S(2)}) copy-start(bf16[4,4,5,4,1,4,256]{6,0,5,3,2,1,4:T(4,128)(2,1)} %copy.35) | copy-start | bytes 1966084
  41.5 5.0 %copy-start.23 = (s32[1,4]{1,0:T(1,128)S(1)}, s32[1,4]{1,0:T(1,128)}, u32[]{:S(2)}) copy-start(s32[1,4]{1,0:T(1,128)} %param.10) | copy-start | bytes 52
  43.0 4.4 %copy-start.22 = (bf16[4,4,5,4,1,4,256]{6,0,5,3,2,1,4:T(4,128)(2,1)S(1)}, bf16[4,4,5,4,1,4,256]{6,0,5,3,2,1,4:T(4,128)(2,1)}, u32[]{:S(2)}) copy-start(bf16[4,4,5,4,1,4,256]{6,0,5,3,2,1,4:T(4,128)(2,1)} %copy.37) | copy-start | bytes 1966084
  48.1 4.8 %copy-start.1 = (bf16[4,4,320,256]{3,2,0,1:T(8,128)(2,1)S(1)}, bf16[4,4,320,256]{3,2,0,1:T(8,128)(2,1)}, u32[]{:S(2)}) copy-start(bf16[4,4,320,256]{3,2,0,1:T(8,128)(2,1)} %copy_multiply_fusion) | copy-start | bytes 7864324
  56.7 1.2 copy-start.20
  58.7 2.5 %copy-start.11 = (bf16[4,4,80,320]{3,2,0,1:T(8,128)(2,1)S(1)}, bf16[4,4,80,320]{3,2,0,1:T(8,128)(2,1)}, u32[]{:S(2)}) copy-start(bf16[4,4,80,320]{3,2,0,1:T(8,128)(2,1)} %copy-done.10) | copy-start | bytes 2457604
  62.1 1.1 copy-start.8
  63.9 1.1 copy-start.6
  66.9 4.8 %collective-permute-start = (f32[4,80,256]{2,1,0:T(8,128)}, f32[4,80,256]{2,1,0:T(8,128)S(1)}, u32[]{:S(2)}, u32[]{:S(2)}) collective-permute-start(f32[4,80,256]{2,1,0:T(8,128)} %convolution_add_fusion.2), channel_id=1, source_target_pairs={{0,8},{8,16},{16,24},{1,9},{9,17},{17,25},{2,10},{10,18},{18,26},{... | collective-permute-start | bytes 983048 | tf_op jit(solution)/shard_map/while/body/eval_jaxpr/ppermute | solution.py:32
  72.9 8.4 %collective-permute-start = (f32[4,80,256]{2,1,0:T(8,128)}, f32[4,80,256]{2,1,0:T(8,128)S(1)}, u32[]{:S(2)}, u32[]{:S(2)}) collective-permute-start(f32[4,80,256]{2,1,0:T(8,128)} %convolution_add_fusion.2), channel_id=1, source_target_pairs={{0,8},{8,16},{16,24},{1,9},{9,17},{17,25},{2,10},{10,18},{18,26},{... | collective-permute-start | bytes 983048 | tf_op jit(solution)/shard_map/while/body/eval_jaxpr/ppermute | solution.py:32
  82.4 8.6 %collective-permute-start = (f32[4,80,256]{2,1,0:T(8,128)}, f32[4,80,256]{2,1,0:T(8,128)S(1)}, u32[]{:S(2)}, u32[]{:S(2)}) collective-permute-start(f32[4,80,256]{2,1,0:T(8,128)} %convolution_add_fusion.2), channel_id=1, source_target_pairs={{0,8},{8,16},{16,24},{1,9},{9,17},{17,25},{2,10},{10,18},{18,26},{... | collective-permute-start | bytes 983048 | tf_op jit(solution)/shard_map/while/body/eval_jaxpr/ppermute | solution.py:32
  91.0 4.4 %copy-start.12 = (bf16[4,4,80,320]{3,2,0,1:T(8,128)(2,1)S(1)}, bf16[4,4,80,320]{3,2,0,1:T(8,128)(2,1)}, u32[]{:S(2)}) copy-start(bf16[4,4,80,320]{3,2,0,1:T(8,128)(2,1)} %copy-done.10) | copy-start | bytes 2457604
  95.5 1.6 copy-start.9
  96.3 2.8 %copy-start.2 = (f32[4,1,320,256]{3,2,0,1:T(8,128)}, f32[4,1,320,256]{3,2,0,1:T(8,128)S(1)}, u32[]{:S(2)}) copy-start(f32[4,1,320,256]{3,2,0,1:T(8,128)S(1)} %fusion.16) | copy-start | bytes 3932164
  96.3 2.0 %copy-start.7 = (f32[4,320,256]{2,1,0:T(8,128)S(1)}, f32[4,320,256]{2,1,0:T(8,128)}, u32[]{:S(2)}) copy-start(f32[4,320,256]{2,1,0:T(8,128)} %copy-done.6) | copy-start | bytes 3932164
  97.1 2.0 %copy-start.3 = (f32[4,1,320,256]{3,2,0,1:T(8,128)}, f32[4,1,320,256]{3,2,0,1:T(8,128)S(1)}, u32[]{:S(2)}) copy-start(f32[4,1,320,256]{3,2,0,1:T(8,128)S(1)} %fusion.18) | copy-start | bytes 3932164
  97.1 2.6 %copy-start = (bf16[4,4,320,256]{3,2,1,0:T(8,128)(2,1)S(1)}, bf16[4,4,320,256]{3,2,1,0:T(8,128)(2,1)}, u32[]{:S(2)}) copy-start(bf16[4,4,320,256]{3,2,1,0:T(8,128)(2,1)} %param.8) | copy-start | bytes 7864324
  98.3 2.9 %copy-start.4 = (f32[4,1,320,256]{3,2,0,1:T(8,128)}, f32[4,1,320,256]{3,2,0,1:T(8,128)S(1)}, u32[]{:S(2)}) copy-start(f32[4,1,320,256]{3,2,0,1:T(8,128)S(1)} %fusion.20) | copy-start | bytes 3932164
  99.7 1.6 copy-start.5
